TPU v7x, 32 devices: a whole 2x2x4 slice. The times are simulated.
32 devices in a mesh: groups: 2 (over y), blk: 4 (over z), heads: 2 (over x), section: 2 (over core).
Axes of the slice: x: 2, y: 2, z: 4, core: 2. Of those that a mesh axis runs over, the one named last changes fastest.
Arguments:
- dec_states: bfloat16 [4096, 2304], P(('groups', 'blk', 'section')), parts along dimension 0, may hold values from -6 to 6
- cross_keys: bfloat16 [1024, 1, 256], P(('groups', 'blk')), parts along dimension 0, may hold values from -15 to 15
- cross_values: bfloat16 [1024, 1, 256], P(('groups', 'blk')), parts along dimension 0, may hold values from -6 to 6
- attn_gain: float32 [2304], replicated, may hold values from 0.1 to 1.9
- query_weight: bfloat16 [2304, 512], P(None, 'heads'), may hold values from -0.125 to 0.125
- out_weight: bfloat16 [512, 2304], P('heads'), may hold values from -0.25 to 0.25
- post_attn_gain: float32 [2304], replicated, may hold values from 0.1 to 1.9
- ffn_gain: float32 [2304], replicated, may hold values from 0.1 to 1.9
- gate_weight: bfloat16 [2304, 9216], P('blk', ('heads', 'section')), may hold values from -0.125 to 0.125
- up_weight: bfloat16 [2304, 9216], P('blk', ('heads', 'section')), may hold values from -0.125 to 0.125
- down_weight: bfloat16 [9216, 2304], P(('heads', 'section'), 'blk'), may hold values from -0.0625 to 0.0625
- post_ffn_gain: float32 [2304], replicated, may hold values from 0.1 to 1.9
Outputs:
- scored_states: bfloat16 [4096, 2304], P(('groups', 'blk', 'heads', 'section')), parts along dimension 0
There are 2 independent parts, one for each index of `groups`. A program takes and returns all parts, laid end to end along the dimension named above; an argument that names none is the same for every part. Nothing has to cross between parts.
All inputs are finite; a program needn't handle non-finite values.
Results may differ from a plain program's by a relative error of at most 0.02.
Values may be sent and summed in bfloat16 or wider, within the bound.
No kernel may reach another device: no remote copies, remote signals or barrier semaphores. Data moves between devices by JAX's collectives and lax.ppermute only.
A program may use at most 128 MiB of HBM per device.

v0:
```python
import jax
import jax.numpy as jnp
from jax import lax
from jax.sharding import PartitionSpec as P

HD = 256
GROUP = 2


softcap_limit = 50.0


def from_partner(block, axis, bit):
    count = lax.axis_size(axis)
    route = []
    for low in range(count):
        high = low | 1 << bit
        if high != low and high < count:
            route += [(low, high), (high, low)]
    return lax.ppermute(block, axis, route)


def rms_scale(values, gain):
    return values * lax.rsqrt(jnp.mean(values * values, axis=-1, keepdims=True) + 1e-06) * gain


def capped_scores(queries, keys):
    raw = lax.dot_general(
        queries, keys, (((1,), (1,)), ((), ())), preferred_element_type=jnp.float32
    ) * HD ** (-0.5)
    return softcap_limit * jnp.tanh(raw / softcap_limit)


def body(
    dec_states,
    cross_keys,
    cross_values,
    attn_gain,
    query_weight,
    out_weight,
    post_attn_gain,
    ffn_gain,
    gate_weight,
    up_weight,
    down_weight,
    post_ffn_gain,
):
    head_index = lax.axis_index("heads")
    kv_index = head_index // GROUP
    keys_local = lax.dynamic_index_in_dim(cross_keys, kv_index, 1, keepdims=False)
    values_local = lax.dynamic_index_in_dim(cross_values, kv_index, 1, keepdims=False)
    gate_full, up_full, down_full = (
        lax.all_gather(gate_weight, "blk", axis=0, tiled=True),
        lax.all_gather(up_weight, "blk", axis=0, tiled=True),
        lax.all_gather(down_weight, "blk", axis=1, tiled=True),
    )
    states = dec_states.astype(jnp.float32)
    normed = rms_scale(states, attn_gain).astype(jnp.bfloat16)
    queries = jnp.dot(normed, query_weight, preferred_element_type=jnp.float32).astype(jnp.bfloat16)
    rows_here = queries.shape[0]
    probs = jnp.exp(capped_scores(queries, lax.all_gather(keys_local, "blk", axis=0, tiled=True)))
    numer = jnp.dot(
        probs.astype(jnp.bfloat16),
        lax.all_gather(values_local, "blk", axis=0, tiled=True),
        preferred_element_type=jnp.float32,
    )
    numer, denom = (numer, jnp.sum(probs, axis=1))
    context = (numer / denom[:, None]).astype(jnp.bfloat16)
    head_term = jnp.dot(context, out_weight, preferred_element_type=jnp.float32)
    attended = lax.psum(head_term.astype(jnp.bfloat16), "heads").astype(jnp.float32)
    residual = (states + rms_scale(attended, post_attn_gain)).astype(jnp.bfloat16)
    ffn_input = rms_scale(residual.astype(jnp.float32), ffn_gain).astype(jnp.bfloat16)
    section_size = lax.axis_size("section")
    section_index = lax.axis_index("section")
    out_rows = rows_here // lax.axis_size("heads")
    block_index = head_index * section_size + section_index
    ffn_rows = lax.all_gather(ffn_input, "section", axis=0, tiled=True)
    partner_block = head_index * section_size + (1 - section_index)
    send_start = jnp.clip(
        partner_block * out_rows - section_index * rows_here, 0, rows_here - out_rows
    )
    outgoing = lax.dynamic_slice_in_dim(residual, send_start, out_rows, 0)
    incoming = from_partner(outgoing, "section", 0)
    own_start = jnp.clip(
        block_index * out_rows - section_index * rows_here, 0, rows_here - out_rows
    )
    local_rows = lax.dynamic_slice_in_dim(residual, own_start, out_rows, 0)
    holder = block_index * out_rows // rows_here
    residual_out = jnp.where(holder == section_index, local_rows, incoming)
    gate = jnp.dot(ffn_rows, gate_full, preferred_element_type=jnp.float32)
    up_part = jnp.dot(ffn_rows, up_full, preferred_element_type=jnp.float32)
    hidden = (jax.nn.gelu(gate, approximate=True) * up_part).astype(jnp.bfloat16)
    terms = jnp.dot(hidden, down_full, preferred_element_type=jnp.float32)
    ffn_out = lax.psum_scatter(
        terms.astype(jnp.bfloat16), ("heads", "section"), scatter_dimension=0, tiled=True
    ).astype(jnp.float32)
    return (residual_out.astype(jnp.float32) + rms_scale(ffn_out, post_ffn_gain)).astype(
        jnp.bfloat16
    )


def solution(mesh):
    in_specs = (
        P(("groups", "blk", "section"), None),
        P(("groups", "blk"), None, None),
        P(("groups", "blk"), None, None),
        P(),
        P(None, "heads"),
        P("heads", None),
        P(),
        P(),
        P("blk", ("heads", "section")),
        P("blk", ("heads", "section")),
        P(("heads", "section"), "blk"),
        P(),
    )
    out_specs = P(("groups", "blk", "heads", "section"), None)
    return jax.shard_map(body, mesh=mesh, in_specs=in_specs, out_specs=out_specs, check_vma=False)
```

profile of v0, /device:TPU:0, one launch (start us, length us, event | category | flops | bytes accessed | tf_op | source)
XLA Modules:
  0.0 725.9 jit_solution(15588221195975664672)
XLA Ops:
  6.5 0.0 copy-start
  6.5 0.0 all-reduce.2.cloned.1.call-start
  6.5 16.0 %all-gather = bf16[512,1,256]{2,0,1:T(8,128)(2,1)S(1)} all-gather(bf16[128,1,256]{2,0,1:T(8,128)(2,1)} %param.13), channel_id=2, replica_groups=mesh['groups'=2,'blk'=4,'heads'=2,'section'=2] {'blk'}, dimensions={0}, use_global_device_ids=true | all-gather | bytes 327680 | tf_op jit(solution)/shard_map/all_gather | solution.py:61
  22.5 1.6 fusion.13
  24.1 14.8 %all-gather.1 = bf16[512,1,256]{2,0,1:T(8,128)(2,1)S(1)} all-gather(bf16[128,1,256]{2,0,1:T(8,128)(2,1)} %param.14), channel_id=3, replica_groups=mesh['groups'=2,'blk'=4,'heads'=2,'section'=2] {'blk'}, dimensions={0}, use_global_device_ids=true | all-gather | bytes 327680 | tf_op jit(solution)/shard_map/all_gather | solution.py:64
  38.9 2.6 fusion.45
  41.4 0.0 copy-done
  41.4 0.0 copy-start.1
  41.5 1.7 convolution_convert_fusion.1
  43.2 0.0 all-reduce.2.cloned.1.call-update
  43.2 0.0 copy-start.2
  43.2 0.0 all-gather.7.cloned.1.call-start
  43.3 43.9 %all-reduce.2.cloned.1.call-done = bf16[256,2304]{1,0:T(8,128)(2,1)} async-done(((bf16[256,2304]{1,0:T(8,128)(2,1)}), bf16[256,2304]{1,0:T(8,128)(2,1)}) %all-reduce.2.cloned.1.call-update) | async-done | bytes 1179664 | tf_op jit(solution)/shard_map/psum | solution.py:70
  87.2 1.6 fusion.8
  88.8 0.0 copy-done.1
  88.8 2.0 fusion.10
  90.8 0.0 copy-done.2
  90.8 1.4 fusion.12
  92.2 0.0 all-gather.7.cloned.1.call-update
  92.2 0.0 all-gather.9.cloned.1.call-start
  92.3 0.7 all-gather.9.cloned.1.call-update
  93.0 0.0 all-gather.11.cloned.1.call-start
  93.0 0.5 all-gather.11.cloned.1.call-update
  93.5 0.0 all-gather.13.cloned.1.call-start
  93.6 0.5 all-gather.13.cloned.1.call-update
  94.1 0.0 reduce-scatter.2.cloned.1.call-start
  94.2 9.2 %all-gather.7.cloned.1.call-done = bf16[512,2304]{1,0:T(8,128)(2,1)} async-done(((bf16[256,2304]{1,0:T(8,128)(2,1)}), bf16[512,2304]{1,0:T(8,128)(2,1)}) %all-gather.7.cloned.1.call-update) | async-done | bytes 2359312 | tf_op jit(solution)/shard_map/all_gather | solution.py:77
  103.3 188.8 %all-gather.9.cloned.1.call-done = bf16[2304,2304]{1,0:T(8,128)(2,1)} async-done(((bf16[576,2304]{1,0:T(8,128)(2,1)}), bf16[2304,2304]{1,0:T(8,128)(2,1)}) %all-gather.9.cloned.1.call-update) | async-done | bytes 10616848 | tf_op jit(solution)/shard_map/all_gather | solution.py:53
  292.2 11.6 %fusion.48 = f32[512,2304]{1,0:T(8,128)} fusion(bf16[512,2304]{1,0:T(8,128)(2,1)} %all-gather.7.cloned.1.call-done, bf16[2304,2304]{1,0:T(8,128)(2,1)} %all-gather.9.cloned.1.call-done), kind=kOutput, calls=%fused_computation.58 | convolution fusion | flops 5435817984 | bytes 17694720 | tf_op jit(solution)/shard_map/dot_general | solution.py:90
  303.8 174.1 %all-gather.11.cloned.1.call-done = bf16[2304,2304]{1,0:T(8,128)(2,1)} async-done(((bf16[576,2304]{1,0:T(8,128)(2,1)}), bf16[2304,2304]{1,0:T(8,128)(2,1)}) %all-gather.11.cloned.1.call-update) | async-done | bytes 10616848 | tf_op jit(solution)/shard_map/all_gather | solution.py:54
  477.8 185.7 %all-gather.13.cloned.1.call-done = bf16[2304,2304]{0,1:T(8,128)(2,1)} async-done(((bf16[2304,576]{0,1:T(8,128)(2,1)}), bf16[2304,2304]{0,1:T(8,128)(2,1)}) %all-gather.13.cloned.1.call-update) | async-done | bytes 10616848 | tf_op jit(solution)/shard_map/all_gather | solution.py:55
  663.5 20.7 %convolution_convert_fusion = bf16[512,2304]{1,0:T(8,128)(2,1)} fusion(bf16[2304,2304]{0,1:T(8,128)(2,1)} %all-gather.13.cloned.1.call-done, bf16[512,2304]{1,0:T(8,128)(2,1)} %all-gather.7.cloned.1.call-done, bf16[2304,2304]{1,0:T(8,128)(2,1)} %all-gather.11.cloned.1.call-done, f32[512,2304]{1,0:T(8,128)} %fusion.48), kind=kOutput, calls=%fused_computation.10 | convolution fusion | flops 10884612096 | bytes 30670848 | tf_op jit(solution)/shard_map/dot_general | solution.py:93
  684.3 0.0 copy-start.3
  684.3 0.0 reduce-scatter.2.cloned.1.call-update
  684.3 0.1 constant_dynamic-slice_fusion
  684.5 0.1 collective-permute-start
  684.6 30.9 %reduce-scatter.2.cloned.1.call-done = bf16[128,2304]{1,0:T(8,128)(2,1)} async-done(((bf16[512,2304]{1,0:T(8,128)(2,1)}), bf16[128,2304]{1,0:T(8,128)(2,1)}) %reduce-scatter.2.cloned.1.call-update) | async-done | bytes 589840 | tf_op jit(solution)/shard_map/reduce_scatter | solution.py:94
  715.4 1.3 fusion.20
  716.7 0.0 collective-permute-done
  716.7 0.0 copy-done.3
  716.7 2.3 fusion.23
  (4 shorter events, 0.0 us)
Async XLA Ops:
  6.5 34.9 %copy-start = (bf16[256,2304]{1,0:T(8,128)(2,1)S(1)}, bf16[256,2304]{1,0:T(8,128)(2,1)}, u32[]{:S(2)}) copy-start(bf16[256,2304]{1,0:T(8,128)(2,1)} %param.17) | copy-start | bytes 3538948
  6.5 80.7 %all-reduce.2.cloned.1.call-start = ((), (), s32[]{:S(2)}) async-start(), calls=%async_computation.1 | async-start | bytes 2359296 | tf_op jit(solution)/shard_map/psum | solution.py:70
  41.4 47.3 %copy-start.1 = (bf16[256,2304]{1,0:T(8,128)(2,1)S(1)}, bf16[256,2304]{1,0:T(8,128)(2,1)}, u32[]{:S(2)}) copy-start(bf16[256,2304]{1,0:T(8,128)(2,1)} %param.12) | copy-start | bytes 3538948
  43.2 47.6 %copy-start.2 = (f32[2304]{0:T(1024)S(1)}, f32[2304]{0:T(1024)}, u32[]{:S(2)}) copy-start(f32[2304]{0:T(1024)} %param.19) | copy-start | bytes 27652
  43.2 60.1 %all-gather.7.cloned.1.call-start = ((), (), s32[]{:S(2)}) async-start(), calls=%async_computation.2 | async-start | bytes 3538944 | tf_op jit(solution)/shard_map/all_gather | solution.py:77
  92.2 199.9 %all-gather.9.cloned.1.call-start = ((), (), s32[]{:S(2)}) async-start(), calls=%async_computation.3 | async-start | bytes 13271040 | tf_op jit(solution)/shard_map/all_gather | solution.py:53
  93.0 384.9 %all-gather.11.cloned.1.call-start = ((), (), s32[]{:S(2)}) async-start(), calls=%async_computation.4 | async-start | bytes 13271040 | tf_op jit(solution)/shard_map/all_gather | solution.py:54
  93.5 570.0 %all-gather.13.cloned.1.call-start = ((), (), s32[]{:S(2)}) async-start(), calls=%async_computation.5 | async-start | bytes 13271040 | tf_op jit(solution)/shard_map/all_gather | solution.py:55
  94.1 621.3 %reduce-scatter.2.cloned.1.call-start = ((), (), s32[]{:S(2)}) async-start(), calls=%async_computation.6 | async-start | bytes 2949120 | tf_op jit(solution)/shard_map/reduce_scatter | solution.py:94
  684.3 32.5 %copy-start.3 = (f32[2304]{0:T(1024)S(1)}, f32[2304]{0:T(1024)}, u32[]{:S(2)}) copy-start(f32[2304]{0:T(1024)} %param.23) | copy-start | bytes 27652
  684.5 32.3 %collective-permute-start = (bf16[128,2304]{1,0:T(8,128)(2,1)S(1)}, bf16[128,2304]{1,0:T(8,128)(2,1)S(1)}, u32[]{:S(2)}, u32[]{:S(2)}) collective-permute-start(bf16[128,2304]{1,0:T(8,128)(2,1)S(1)} %constant_dynamic-slice_fusion), channel_id=1, source_target_pairs={{0,1},{1,0},{2,3},{3,2},{4,5},{5,4},{6,7},{7,6},{8,9},{9,8},{10,11... | collective-permute-start | bytes 1769480 | tf_op jit(solution)/shard_map/ppermute | solution.py:20
Sparse Core Ops, SparseCore 0:
  43.3 43.8 all-reduce.1
  92.3 10.9 all-gather.6
  104.9 187.2 all-gather.8
  293.6 184.2 all-gather.10
  479.3 184.2 all-gather.12
  684.4 30.9 reduce-scatter.1
where the time goes:
time: 726 us
  waiting for transfers between devices  634 us (87%)
  matrix products  36.7 us (5%)
  blocking collectives  30.7 us (4%)
  between operations  13.6 us (2%)
  other arithmetic  10.1 us (1%)
    all_gather x1, waiting for transfers between devices, body(): lax.all_gather(gate_weight, 'blk', axis=0, tiled=True)  189 us
    all_gather x1, waiting for transfers between devices, body(): lax.all_gather(down_weight, 'blk', axis=1, tiled=True)  186 us
    all_gather x1, waiting for transfers between devices, body(): lax.all_gather(up_weight, 'blk', axis=0, tiled=True)  174 us
    psum x1, waiting for transfers between devices, body(): lax.psum(head_term.astype(jnp.bfloat16), 'heads').astype(jnp.float32)  43.9 us
    reduce_scatter x1, waiting for transfers between devices, body(): lax.psum_scatter(terms.astype(jnp.bfloat16), ('heads', 'section'), scatte...  30.9 us
    dot_general x1, matrix products, body(): terms = jnp.dot(hidden, down_full, preferred_element_type=jnp.float32)  20.7 us
    all_gather x1, blocking collectives, body(): lax.all_gather(keys_local, 'blk', axis=0, tiled=True)  16 us
    all_gather x1, blocking collectives, body(): lax.all_gather(values_local, 'blk', axis=0, tiled=True)  14.8 us
  transfers between devices with their start and end apart: 7, of which 6 were waited for; matrix products, arithmetic and copies ran while one was open for 2% of the time, Pallas kernels for 0%

commit v1 on v0

--- a/solution.py
+++ b/solution.py
@@ -1,10 +1,14 @@
 import jax
 import jax.numpy as jnp
 from jax import lax
+from jax.experimental import pallas as pl
+from jax.experimental.pallas import tpu as pltpu
 from jax.sharding import PartitionSpec as P
+
 
 HD = 256
 GROUP = 2
+LANE = 128
 
 
 softcap_limit = 50.0
@@ -31,7 +35,7 @@
     return softcap_limit * jnp.tanh(raw / softcap_limit)
 
 
-def body(
+def gathered_body(
     dec_states,
     cross_keys,
     cross_values,
@@ -99,6 +103,165 @@
     )
 
 
+def shifted(block, axis, step):
+    count = lax.axis_size(axis)
+    return lax.ppermute(block, axis, [(i, (i + step) % count) for i in range(count)])
+
+
+def ffn_kernel(rows_ref, weights_ref, out_ref, hidden_ref):
+    rows = rows_ref[...]
+    _, width, units = weights_ref.shape
+    for at in range(0, units, TILE):
+        to = min(at + TILE, units)
+        gate = jnp.dot(rows, weights_ref[0, :, at:to], preferred_element_type=jnp.float32)
+        up_part = jnp.dot(rows, weights_ref[1, :, at:to], preferred_element_type=jnp.float32)
+        hidden_ref[:, at:to] = (jax.nn.gelu(gate, approximate=True) * up_part).astype(jnp.bfloat16)
+    hidden = hidden_ref[...]
+    for at in range(0, width, TILE):
+        to = min(at + TILE, width)
+        out_ref[:, at:to] = lax.dot_general(
+            hidden,
+            weights_ref[2, at:to, :],
+            (((1,), (1,)), ((), ())),
+            preferred_element_type=jnp.float32,
+        ).astype(jnp.bfloat16)
+
+
+def ffn(rows, weights):
+    _, width, units = weights.shape
+    count = rows.shape[0]
+    in_vmem = pl.BlockSpec(memory_space=pltpu.VMEM)
+    return pl.pallas_call(
+        ffn_kernel,
+        out_shape=jax.ShapeDtypeStruct((count, width), jnp.bfloat16),
+        in_specs=[in_vmem, in_vmem],
+        out_specs=in_vmem,
+        scratch_shapes=[pltpu.VMEM((count, units), jnp.bfloat16)],
+        cost_estimate=pl.CostEstimate(
+            flops=6 * count * width * units,
+            bytes_accessed=4 * count * width,
+            transcendentals=count * units,
+        ),
+        compiler_params=pltpu.CompilerParams(vmem_limit_bytes=40 << 20),
+        name="ffn",
+    )(rows, weights)
+
+
+TILE = 256
+TURNS = (2, 1, 3)
+
+
+def exchanged_body(
+    dec_states,
+    cross_keys,
+    cross_values,
+    attn_gain,
+    query_weight,
+    out_weight,
+    post_attn_gain,
+    ffn_gain,
+    gate_weight,
+    up_weight,
+    down_weight,
+    post_ffn_gain,
+):
+    blks = lax.axis_size("blk")
+    g, z, h, c = (lax.axis_index(axis) for axis in ("groups", "blk", "heads", "section"))
+    f32, bf16 = jnp.float32, jnp.bfloat16
+
+    kv_index = h // GROUP
+    keys_local = lax.dynamic_index_in_dim(cross_keys, kv_index, 1, keepdims=False)
+    values_local = lax.dynamic_index_in_dim(cross_values, kv_index, 1, keepdims=False)
+    mine = jnp.where(c == 0, keys_local, values_local)
+    mine = jnp.concatenate([mine] + [shifted(mine, "blk", d) for d in range(1, blks)], axis=0)
+    other = shifted(mine, "section", 1)
+    keys = jnp.where(c == 0, mine, other)
+    values = jnp.where(c == 0, other, mine)
+
+    depth, units = gate_weight.shape
+    piece = 2 * units // blks
+    share = depth // 4
+    weights = (gate_weight, up_weight, down_weight.T)
+
+    def cut(row, rows, column, columns):
+        return jnp.stack(
+            [lax.dynamic_slice(w, (row, column), (rows, columns)) for w in weights]
+        )
+
+    own_quarter = cut((2 * g + c) * share, share, 0, units)
+    next_quarter = shifted(cut((2 * g + 1 - c) * share, share, 0, units), "section", 1)
+    low = jnp.where(c == 0, own_quarter, next_quarter)
+    high = jnp.where(c == 0, next_quarter, own_quarter)
+
+    def quarter_for(target):
+        column = target % (blks // 2) * piece
+        cuts = [lax.dynamic_slice_in_dim(part, column, piece, 2) for part in (low, high)]
+        return jnp.where(target < blks // 2, *cuts)
+
+    full = jnp.zeros((3, blks * depth, piece), bf16)
+
+    def put(part, row):
+        nonlocal full
+        full = lax.dynamic_update_slice(full, part, (0, row, 0))
+
+    here = cut(0, depth, z % (blks // 2) * piece, piece)
+    hand_over = [(2 * b + b // (blks // 2), 2 * b + 1 - b // (blks // 2)) for b in range(blks)]
+    passed = lax.ppermute(here, ("blk", "section"), hand_over)
+    put(jnp.where(z // (blks // 2) == c, here, passed), z * depth)
+    for step in TURNS:
+        row = (z - step) % blks * depth
+        part = shifted(quarter_for((z + step) % blks), "blk", step)
+        across = shifted(part, "groups", 1)
+        put(part, row + (2 * g + c) * share)
+        put(shifted(part, "section", 1), row + (2 * g + 1 - c) * share)
+        put(across, row + (2 * (1 - g) + c) * share)
+        put(shifted(across, "section", 1), row + (2 * (1 - g) + 1 - c) * share)
+
+    states = dec_states.astype(f32)
+    normed = rms_scale(states, attn_gain).astype(bf16)
+    queries = jnp.dot(normed, query_weight, preferred_element_type=f32).astype(bf16)
+    probs = jnp.exp(capped_scores(queries, keys))
+    numer = jnp.dot(probs.astype(bf16), values, preferred_element_type=f32)
+    context = (numer / jnp.sum(probs, axis=1)[:, None]).astype(bf16)
+    head_term = jnp.dot(context, out_weight, preferred_element_type=f32).astype(bf16)
+    attended = head_term.astype(f32) + shifted(head_term, "heads", 1).astype(f32)
+    residual = (states + rms_scale(attended, post_attn_gain)).astype(bf16)
+    ffn_input = rms_scale(residual.astype(f32), ffn_gain).astype(bf16)
+
+    rows_here = dec_states.shape[0]
+    half = rows_here // 2
+    own_half = lax.dynamic_slice_in_dim(ffn_input, h * half, half, 0)
+    chunks = {0: ffn_input}
+    for d in TURNS:
+        mine = shifted(own_half, "blk", -d)
+        other = shifted(mine, "heads", 1)
+        chunks[d] = jnp.concatenate([jnp.where(h == 0, mine, other), jnp.where(h == 0, other, mine)])
+
+    to_keeper = [(2 * (1 - core) + core, 2 * core + core) for core in range(2)]
+    ffn_out = 0.0
+    for d in (0, *TURNS):
+        terms = ffn(chunks[d], full)
+        total = terms.astype(f32)
+        total += lax.ppermute(terms, ("heads", "section"), to_keeper).astype(f32)
+        if d > 0:
+            route = [
+                ((b * 2 + core) * 2 + core, ((b + d) % blks * 2 + core) * 2 + core)
+                for b in range(blks)
+                for core in range(2)
+            ]
+            total = lax.ppermute(total.astype(bf16), ("blk", "heads", "section"), route)
+            total = total.astype(f32)
+        ffn_out += total
+    scored = (residual.astype(f32) + rms_scale(ffn_out, post_ffn_gain)).astype(bf16)
+    halves = lax.dynamic_slice_in_dim(scored, c * half, half, 0)
+    handed = lax.ppermute(
+        lax.dynamic_slice_in_dim(scored, (1 - c) * half, half, 0),
+        ("heads", "section"),
+        [(2 * core + core, 2 * core + 1 - core) for core in range(2)],
+    )
+    return jnp.where(h == c, halves, handed)
+
+
 def solution(mesh):
     in_specs = (
         P(("groups", "blk", "section"), None),
@@ -115,4 +278,26 @@
         P(),
     )
     out_specs = P(("groups", "blk", "heads", "section"), None)
-    return jax.shard_map(body, mesh=mesh, in_specs=in_specs, out_specs=out_specs, check_vma=False)
+
+    def program(*args):
+        sizes = dict(mesh.shape)
+        gate_weight = args[8]
+        units = gate_weight.shape[1] // (sizes["heads"] * sizes["section"])
+        depth = gate_weight.shape[0] // sizes["blk"]
+        fits = (
+            sizes["groups"] == sizes["heads"] == sizes["section"] == 2
+            and sizes["blk"] == 1 + len(TURNS)
+            and depth % (4 * 16) == 0
+            and 2 * units % (LANE * sizes["blk"]) == 0
+        )
+        if not fits:
+            return jax.shard_map(
+                gathered_body, mesh=mesh, in_specs=in_specs, out_specs=out_specs, check_vma=False
+            )(*args)
+
+        step = jax.shard_map(
+            exchanged_body, mesh=mesh, in_specs=in_specs, out_specs=out_specs, check_vma=False
+        )
+        return step(*args)
+
+    return program

time: 726 us -> 360 us (0.50)
  waiting for transfers between devices: 634 us -> 174 us
  starting transfers between devices: 0.27 us -> 95.1 us
  Pallas kernels: 0 us -> 41.8 us
  matrix products: 36.7 us -> 4.31 us
  blocking collectives: 30.7 us -> 0 us
  other arithmetic: 10.1 us -> 27.6 us
  local copies, waits for them, and re-layouts: 0.17 us -> 15.8 us
  between operations: 13.6 us -> 0.66 us
    all_gather x4 -> x0, waiting for transfers between devices: 558 us -> none  [the longest x1 189 us: body(): lax.all_gather(gate_weight, 'blk', axis=0, tiled=True)]
    ppermute x1 -> x33, waiting for transfers between devices: 0.01 us -> 174 us  [the longest x24 127 us: shifted(): lax.ppermute(block, axis, [(i, (i + step) % count) for i in range(count)])]
    ppermute x1 -> x33, starting transfers between devices: 0.07 us -> 95.1 us  [the longest x24 76.3 us: shifted(): lax.ppermute(block, axis, [(i, (i + step) % count) for i in range(count)])]
    psum x1 -> x0, waiting for transfers between devices: 43.9 us -> none  [body(): lax.psum(head_term.astype(jnp.bfloat16), 'heads').astype(jnp.float32)]
    pallas_call x0 -> x4, Pallas kernels: none -> 41.8 us  [ffn(): pl.pallas_call(ffn_kernel, out_shape=jax.ShapeDtypeStruct((count, width),...]
    dot_general x3 -> x1, matrix products: 34.1 us -> 1.74 us  [exchanged_body(): jnp.dot(context, out_weight, preferred_element_type=f32).astype(bf16)]
    reduce_scatter x1 -> x0, waiting for transfers between devices: 30.9 us -> none  [body(): lax.psum_scatter(terms.astype(jnp.bfloat16), ('heads', 'section'), scatte...]
    all_gather x2 -> x0, blocking collectives: 30.7 us -> none  [the longest x1 16 us: body(): lax.all_gather(keys_local, 'blk', axis=0, tiled=True)]
  transfers between devices with their start and end apart: 7 -> 33, of which waited for: 6 -> 17; matrix products, arithmetic and copies ran while one was open for 2% -> 8% of each run, Pallas kernels for 0% -> 9%
where the time goes in v1:
time: 360 us; the launch traced here: 359 us
  waiting for transfers between devices  174 us (48%)
  starting transfers between devices  95.1 us (26%)
  Pallas kernels  41.8 us (12%)
  other arithmetic  27.6 us (8%)
  local copies, waits for them, and re-layouts  15.8 us (4%)
  matrix products  4.31 us (1%)
    ppermute x24, waiting for transfers between devices, shifted(): lax.ppermute(block, axis, [(i, (i + step) % count) for i in range(count)])  127 us
    ppermute x24, starting transfers between devices, shifted(): lax.ppermute(block, axis, [(i, (i + step) % count) for i in range(count)])  76.3 us
    pallas_call x4, Pallas kernels, ffn(): pl.pallas_call(ffn_kernel, out_shape=jax.ShapeDtypeStruct((count, width),...  41.8 us
    ppermute x3, waiting for transfers between devices, exchanged_body(): total = lax.ppermute(total.astype(bf16), ('blk', 'heads', 'section'), route)  34.3 us
    ppermute x4, waiting for transfers between devices, exchanged_body(): total += lax.ppermute(terms, ('heads', 'section'), to_keeper).astype(f32)  10.9 us
    ppermute x3, starting transfers between devices, exchanged_body(): total = lax.ppermute(total.astype(bf16), ('blk', 'heads', 'section'), route)  8.31 us
    reduce_sum x4, other arithmetic, rms_scale(): jnp.mean(values * values, axis=-1, keepdims=True) + 1e-06  8 us
  transfers between devices with their start and end apart: 33, of which 17 were waited for; matrix products, arithmetic and copies ran while one was open for 8% of the time, Pallas kernels for 9%

profile of v1, /device:TPU:0, one launch (start us, length us, event | category | flops | bytes accessed | tf_op | source)
XLA Modules:
  0.0 359.2 jit_solution(631054642755554921)
XLA Ops:
  0.0 0.9 select_bitcast_fusion
  1.0 3.1 collective-permute-start
  4.1 2.6 collective-permute-start.1
  6.6 1.3 collective-permute-start.2
  8.5 2.6 collective-permute-done.1
  11.5 1.6 fusion
  13.1 2.6 fusion.31
  15.7 1.7 convolution_convert_fusion
  17.4 1.5 collective-permute-start.4
  18.9 1.4 dynamic-slice_bitcast_fusion.6
  20.3 2.6 dynamic-slice_bitcast_fusion.7
  22.8 1.6 pad_maximum_fusion.2
  24.7 1.9 dynamic-slice_bitcast_fusion.1
  26.7 19.3 %collective-permute-done.4 = bf16[256,2304]{1,0:T(8,128)(2,1)S(1)} collective-permute-done((bf16[256,2304]{1,0:T(8,128)(2,1)}, bf16[256,2304]{1,0:T(8,128)(2,1)S(1)}, u32[]{:S(2)}, u32[]{:S(2)}) %collective-permute-start.4) | collective-permute-done | bytes 1179680 | tf_op jit(solution)/shard_map/ppermute | solution.py:108
  46.0 1.7 multiply_reduce_fusion.1
  47.8 2.1 fusion.4
  50.3 0.9 constant_dynamic-slice_fusion
  52.4 2.3 pad_maximum_fusion
  54.7 3.5 collective-permute-start.5
  58.2 1.1 collective-permute-start.24
  59.3 1.1 collective-permute-start.28
  60.4 21.9 %collective-permute-done.20 = bf16[128,2304]{1,0:T(8,128)(2,1)} collective-permute-done((bf16[128,2304]{1,0:T(8,128)(2,1)}, bf16[128,2304]{1,0:T(8,128)(2,1)}, u32[]{:S(2)}, u32[]{:S(2)}) %collective-permute-start.20) | collective-permute-done | bytes 589856 | tf_op jit(solution)/shard_map/ppermute | solution.py:108
  82.3 1.5 collective-permute-start.21
  83.8 2.2 broadcast_select_fusion.1
  86.9 9.1 %collective-permute-done.24 = bf16[128,2304]{1,0:T(8,128)(2,1)S(1)} collective-permute-done((bf16[128,2304]{1,0:T(8,128)(2,1)}, bf16[128,2304]{1,0:T(8,128)(2,1)S(1)}, u32[]{:S(2)}, u32[]{:S(2)}) %collective-permute-start.24) | collective-permute-done | bytes 589856 | tf_op jit(solution)/shard_map/ppermute | solution.py:108
  96.0 53.4 %collective-permute-start.11 = (bf16[3,144,1152]{2,1,0:T(8,128)(2,1)S(1)}, bf16[3,144,1152]{2,1,0:T(8,128)(2,1)S(1)}, u32[]{:S(2)}, u32[]{:S(2)}) collective-permute-start(bf16[3,144,1152]{2,1,0:T(8,128)(2,1)S(1)} %get-tuple-element.8), channel_id=1, source_target_pairs={{0,4},{4,8},{8,12},{12,0},{1,5},{5,9},{9,13},{13,1},{2,6},{6,10},{... | collective-permute-start | bytes 2985992 | tf_op jit(solution)/shard_map/ppermute | solution.py:108
  149.4 1.5 collective-permute-start.25
  150.9 1.1 broadcast_select_fusion.7
  152.3 10.6 %collective-permute-done.25 = bf16[128,2304]{1,0:T(8,128)(2,1)S(1)} collective-permute-done((bf16[128,2304]{1,0:T(8,128)(2,1)S(1)}, bf16[128,2304]{1,0:T(8,128)(2,1)S(1)}, u32[]{:S(2)}, u32[]{:S(2)}) %collective-permute-start.25) | collective-permute-done | bytes 589856 | tf_op jit(solution)/shard_map/ppermute | solution.py:108
  162.9 1.5 collective-permute-start.29
  164.7 5.6 %collective-permute-done.7 = bf16[3,144,1152]{2,1,0:T(8,128)(2,1)S(1)} collective-permute-done((bf16[3,144,1152]{2,1,0:T(8,128)(2,1)S(1)}, bf16[3,144,1152]{2,1,0:T(8,128)(2,1)S(1)}, u32[]{:S(2)}, u32[]{:S(2)}) %collective-permute-start.7) | collective-permute-done | bytes 995360 | tf_op jit(solution)/shard_map/ppermute | solution.py:108
  170.2 1.5 collective-permute-start.9
  171.8 3.1 collective-permute-done.29
  175.6 14.8 %collective-permute-done.15 = bf16[3,144,1152]{2,1,0:T(8,128)(2,1)S(1)} collective-permute-done((bf16[3,144,1152]{2,1,0:T(8,128)(2,1)S(1)}, bf16[3,144,1152]{2,1,0:T(8,128)(2,1)S(1)}, u32[]{:S(2)}, u32[]{:S(2)}) %collective-permute-start.15) | collective-permute-done | bytes 995360 | tf_op jit(solution)/shard_map/ppermute | solution.py:108
  190.4 1.5 collective-permute-start.13
  192.5 1.3 broadcast_in_dim.2
  193.8 1.3 select_dynamic-update-slice_fusion
  195.2 2.1 collective-permute-start.16
  197.3 18.0 %collective-permute-done.13 = bf16[3,144,1152]{2,1,0:T(8,128)(2,1)S(1)} collective-permute-done((bf16[3,144,1152]{2,1,0:T(8,128)(2,1)S(1)}, bf16[3,144,1152]{2,1,0:T(8,128)(2,1)S(1)}, u32[]{:S(2)}, u32[]{:S(2)}) %collective-permute-start.13) | collective-permute-done | bytes 995360 | tf_op jit(solution)/shard_map/ppermute | solution.py:108
  215.3 20.4 %collective-permute-done.17 = bf16[3,144,1152]{2,1,0:T(8,128)(2,1)S(1)} collective-permute-done((bf16[3,144,1152]{2,1,0:T(8,128)(2,1)S(1)}, bf16[3,144,1152]{2,1,0:T(8,128)(2,1)S(1)}, u32[]{:S(2)}, u32[]{:S(2)}) %collective-permute-start.17) | collective-permute-done | bytes 995360 | tf_op jit(solution)/shard_map/ppermute | solution.py:108
  237.3 1.0 collective-permute-done.18
  238.4 5.5 %copy-done.2 = bf16[3,2304,1152]{2,1,0:T(8,128)(2,1)} copy-done((bf16[3,2304,1152]{2,1,0:T(8,128)(2,1)}, bf16[3,2304,1152]{2,1,0:T(8,128)(2,1)S(1)}, u32[]{:S(2)}) %copy-start.2) | copy-done | bytes 15925272
  244.0 10.4 %ffn.5 = bf16[256,2304]{1,0:T(8,128)(2,1)S(1)} custom-call(bf16[256,2304]{1,0:T(8,128)(2,1)S(1)} %pad_maximum_fusion.3.rows_ref, bf16[3,2304,1152]{2,1,0:T(8,128)(2,1)} %copy-done.2), custom_call_target="tpu_custom_call" | custom-call | flops 4076863488 | bytes 2359296 | tf_op jit(solution)/shard_map/ffn/pallas_call | solution.py:134
  254.4 1.5 collective-permute-start.22
  256.0 10.4 %ffn.6 = bf16[256,2304]{1,0:T(8,128)(2,1)S(1)} custom-call(bf16[256,2304]{1,0:T(8,128)(2,1)S(1)} %pad_maximum_fusion.4.rows_ref, bf16[3,2304,1152]{2,1,0:T(8,128)(2,1)} %copy-done.2), custom_call_target="tpu_custom_call" | custom-call | flops 4076863488 | bytes 2359296 | tf_op jit(solution)/shard_map/ffn/pallas_call | solution.py:134
  266.5 1.3 collective-permute-start.26
  267.8 10.4 %ffn.4 = bf16[256,2304]{1,0:T(8,128)(2,1)S(1)} custom-call(bf16[256,2304]{1,0:T(8,128)(2,1)S(1)} %fusion.6.rows_ref, bf16[3,2304,1152]{2,1,0:T(8,128)(2,1)} %copy-done.2), custom_call_target="tpu_custom_call" | custom-call | flops 4076863488 | bytes 2359296 | tf_op jit(solution)/shard_map/ffn/pallas_call | solution.py:134
  278.2 1.6 collective-permute-start.19
  279.8 10.4 %ffn.7 = bf16[256,2304]{1,0:T(8,128)(2,1)S(1)} custom-call(bf16[256,2304]{1,0:T(8,128)(2,1)S(1)} %pad_maximum_fusion.5.rows_ref, bf16[3,2304,1152]{2,1,0:T(8,128)(2,1)} %copy-done.2), custom_call_target="tpu_custom_call" | custom-call | flops 4076863488 | bytes 2359296 | tf_op jit(solution)/shard_map/ffn/pallas_call | solution.py:134
  290.2 1.3 collective-permute-start.30
  291.5 1.3 add_convert_fusion.2
  292.8 1.9 collective-permute-start.23
  294.8 1.3 add_convert_fusion.1
  296.1 3.5 collective-permute-start.27
  299.6 10.9 %collective-permute-done.30 = bf16[256,2304]{1,0:T(8,128)(2,1)S(1)} collective-permute-done((bf16[256,2304]{1,0:T(8,128)(2,1)S(1)}, bf16[256,2304]{1,0:T(8,128)(2,1)S(1)}, u32[]{:S(2)}, u32[]{:S(2)}) %collective-permute-start.30) | collective-permute-done | bytes 1179680 | tf_op jit(solution)/shard_map/ppermute | solution.py:245
  310.4 1.4 add_convert_fusion
  311.8 2.9 collective-permute-start.31
  314.8 21.6 %collective-permute-done.23 = bf16[256,2304]{1,0:T(8,128)(2,1)S(1)} collective-permute-done((bf16[256,2304]{1,0:T(8,128)(2,1)}, bf16[256,2304]{1,0:T(8,128)(2,1)S(1)}, u32[]{:S(2)}, u32[]{:S(2)}) %collective-permute-start.23) | collective-permute-done | bytes 1179680 | tf_op jit(solution)/shard_map/ppermute | solution.py:252
  336.5 12.6 %collective-permute-done.31 = bf16[256,2304]{1,0:T(8,128)(2,1)} collective-permute-done((bf16[256,2304]{1,0:T(8,128)(2,1)}, bf16[256,2304]{1,0:T(8,128)(2,1)}, u32[]{:S(2)}, u32[]{:S(2)}) %collective-permute-start.31) | collective-permute-done | bytes 1179680 | tf_op jit(solution)/shard_map/ppermute | solution.py:252
  349.1 2.5 multiply_reduce_fusion
  351.7 3.6 fusion.7
  355.3 1.3 collective-permute-start.32
  356.6 1.6 collective-permute-done.32
  358.2 1.0 dynamic-slice_select_fusion.3
  (88 shorter events, 7.3 us)
Async XLA Ops:
  0.0 15.6 %copy-start = (bf16[256,2304]{1,0:T(8,128)(2,1)S(1)}, bf16[256,2304]{1,0:T(8,128)(2,1)}, u32[]{:S(2)}) copy-start(bf16[256,2304]{1,0:T(8,128)(2,1)} %param.17) | copy-start | bytes 3538948
  1.0 7.6 %collective-permute-start = (bf16[128,256]{1,0:T(8,128)(2,1)S(1)}, bf16[128,256]{1,0:T(8,128)(2,1)S(1)}, u32[]{:S(2)}, u32[]{:S(2)}) collective-permute-start(bf16[128,256]{1,0:T(8,128)(2,1)S(1)} %select_bitcast_fusion), channel_id=1, source_target_pairs={{0,4},{4,8},{8,12},{12,0},{1,5},{5,9},{9,13},{13,1},{2,6},{6,10},{... | collective-permute-start | bytes 196616 | tf_op jit(solution)/shard_map/ppermute | solution.py:108
  4.1 7.1 %collective-permute-start.1 = (bf16[128,256]{1,0:T(8,128)(2,1)S(1)}, bf16[128,256]{1,0:T(8,128)(2,1)S(1)}, u32[]{:S(2)}, u32[]{:S(2)}) collective-permute-start(bf16[128,256]{1,0:T(8,128)(2,1)S(1)} %select_bitcast_fusion), channel_id=1, source_target_pairs={{0,8},{4,12},{8,0},{12,4},{1,9},{5,13},{9,1},{13,5},{2,10},{6,14},... | collective-permute-start | bytes 196616 | tf_op jit(solution)/shard_map/ppermute | solution.py:108
  6.6 4.7 %collective-permute-start.2 = (bf16[128,256]{1,0:T(8,128)(2,1)S(1)}, bf16[128,256]{1,0:T(8,128)(2,1)S(1)}, u32[]{:S(2)}, u32[]{:S(2)}) collective-permute-start(bf16[128,256]{1,0:T(8,128)(2,1)S(1)} %select_bitcast_fusion), channel_id=1, source_target_pairs={{0,12},{4,0},{8,4},{12,8},{1,13},{5,1},{9,5},{13,9},{2,14},{6,2},{... | collective-permute-start | bytes 196616 | tf_op jit(solution)/shard_map/ppermute | solution.py:108
  11.4 1.7 collective-permute-start.3
  17.4 2.9 copy-start.13
  17.4 28.6 %collective-permute-start.4 = (bf16[256,2304]{1,0:T(8,128)(2,1)}, bf16[256,2304]{1,0:T(8,128)(2,1)S(1)}, u32[]{:S(2)}, u32[]{:S(2)}) collective-permute-start(bf16[256,2304]{1,0:T(8,128)(2,1)} %convolution_convert_fusion), channel_id=1, source_target_pairs={{0,2},{2,0},{1,3},{3,1},{4,6},{6,4},{5,7},{7,5},{8,10},{10,8},{9,1... | collective-permute-start | bytes 3538952 | tf_op jit(solution)/shard_map/ppermute | solution.py:108
  24.5 59.4 %collective-permute-start.6 = (bf16[3,144,2304]{2,1,0:T(8,128)(2,1)}, bf16[3,144,2304]{2,1,0:T(8,128)(2,1)}, u32[]{:S(2)}, u32[]{:S(2)}) collective-permute-start(bf16[3,144,2304]{2,1,0:T(8,128)(2,1)} %pad_maximum_fusion.2), channel_id=1, source_target_pairs={{0,1},{1,0},{2,3},{3,2},{4,5},{5,4},{6,7},{7,6},{8,9},{9,8},{10,11... | collective-permute-start | bytes 5971976 | tf_op jit(solution)/shard_map/ppermute | solution.py:108
  26.7 25.8 %copy-start.3 = (bf16[1,576,1152]{2,1,0:T(8,128)(2,1)}, bf16[1,576,1152]{2,1,0:T(8,128)(2,1)S(1)}, u32[]{:S(2)}) copy-start(bf16[1,576,1152]{2,1,0:T(8,128)(2,1)S(1)} %get-tuple-element.27) | copy-start | bytes 3981316
  26.7 21.1 %copy-start.11 = (bf16[256,2304]{1,0:T(8,128)(2,1)S(1)}, bf16[256,2304]{1,0:T(8,128)(2,1)}, u32[]{:S(2)}) copy-start(bf16[256,2304]{1,0:T(8,128)(2,1)} %param.12) | copy-start | bytes 3538948
  26.7 21.1 %copy-start.14 = (f32[2304]{0:T(1024)S(1)}, f32[2304]{0:T(1024)}, u32[]{:S(2)}) copy-start(f32[2304]{0:T(1024)} %param.18) | copy-start | bytes 27652
  47.8 2.2 copy-start.15
  49.9 1.3 copy-start.7
  49.9 2.4 copy-start.12
  51.2 31.2 %collective-permute-start.20 = (bf16[128,2304]{1,0:T(8,128)(2,1)}, bf16[128,2304]{1,0:T(8,128)(2,1)}, u32[]{:S(2)}, u32[]{:S(2)}) collective-permute-start(bf16[128,2304]{1,0:T(8,128)(2,1)} %constant_dynamic-slice_fusion), channel_id=1, source_target_pairs={{0,8},{4,12},{8,0},{12,4},{1,9},{5,13},{9,1},{13,5},{2,10},{6,14},... | collective-permute-start | bytes 1769480 | tf_op jit(solution)/shard_map/ppermute | solution.py:108
  52.4 2.3 copy-start.5
  54.7 137.2 %collective-permute-start.5 = (bf16[3,576,1152]{2,1,0:T(8,128)(2,1)}, bf16[3,576,1152]{2,1,0:T(8,128)(2,1)}, u32[]{:S(2)}, u32[]{:S(2)}) collective-permute-start(bf16[3,576,1152]{2,1,0:T(8,128)(2,1)} %pad_maximum_fusion), channel_id=1, source_target_pairs={{0,1},{4,5},{9,8},{13,12},{2,3},{6,7},{11,10},{15,14},{16,17},{20,... | collective-permute-start | bytes 11943944 | tf_op jit(solution)/shard_map/ppermute | solution.py:209
  58.2 37.8 %collective-permute-start.24 = (bf16[128,2304]{1,0:T(8,128)(2,1)}, bf16[128,2304]{1,0:T(8,128)(2,1)S(1)}, u32[]{:S(2)}, u32[]{:S(2)}) collective-permute-start(bf16[128,2304]{1,0:T(8,128)(2,1)} %constant_dynamic-slice_fusion), channel_id=1, source_target_pairs={{0,12},{4,0},{8,4},{12,8},{1,13},{5,1},{9,5},{13,9},{2,14},{6,2},{... | collective-permute-start | bytes 1769480 | tf_op jit(solution)/shard_map/ppermute | solution.py:108
  59.3 92.7 %collective-permute-start.28 = (bf16[128,2304]{1,0:T(8,128)(2,1)}, bf16[128,2304]{1,0:T(8,128)(2,1)S(1)}, u32[]{:S(2)}, u32[]{:S(2)}) collective-permute-start(bf16[128,2304]{1,0:T(8,128)(2,1)} %constant_dynamic-slice_fusion), channel_id=1, source_target_pairs={{0,4},{4,8},{8,12},{12,0},{1,5},{5,9},{9,13},{13,1},{2,6},{6,10},{... | collective-permute-start | bytes 1769480 | tf_op jit(solution)/shard_map/ppermute | solution.py:108
  82.3 67.1 %collective-permute-start.21 = (bf16[128,2304]{1,0:T(8,128)(2,1)}, bf16[128,2304]{1,0:T(8,128)(2,1)S(1)}, u32[]{:S(2)}, u32[]{:S(2)}) collective-permute-start(bf16[128,2304]{1,0:T(8,128)(2,1)} %collective-permute-done.20), channel_id=1, source_target_pairs={{0,2},{2,0},{1,3},{3,1},{4,6},{6,4},{5,7},{7,5},{8,10},{10,8},{9,1... | collective-permute-start | bytes 1769480 | tf_op jit(solution)/shard_map/ppermute | solution.py:108
  86.8 83.4 %collective-permute-start.7 = (bf16[3,144,1152]{2,1,0:T(8,128)(2,1)S(1)}, bf16[3,144,1152]{2,1,0:T(8,128)(2,1)S(1)}, u32[]{:S(2)}, u32[]{:S(2)}) collective-permute-start(bf16[3,144,1152]{2,1,0:T(8,128)(2,1)S(1)} %get-tuple-element.9), channel_id=1, source_target_pairs={{0,8},{4,12},{8,0},{12,4},{1,9},{5,13},{9,1},{13,5},{2,10},{6,14},... | collective-permute-start | bytes 2985992 | tf_op jit(solution)/shard_map/ppermute | solution.py:108
  96.0 79.1 %collective-permute-start.11 = (bf16[3,144,1152]{2,1,0:T(8,128)(2,1)S(1)}, bf16[3,144,1152]{2,1,0:T(8,128)(2,1)S(1)}, u32[]{:S(2)}, u32[]{:S(2)}) collective-permute-start(bf16[3,144,1152]{2,1,0:T(8,128)(2,1)S(1)} %get-tuple-element.8), channel_id=1, source_target_pairs={{0,4},{4,8},{8,12},{12,0},{1,5},{5,9},{9,13},{13,1},{2,6},{6,10},{... | collective-permute-start | bytes 2985992 | tf_op jit(solution)/shard_map/ppermute | solution.py:108
  149.4 13.5 %collective-permute-start.25 = (bf16[128,2304]{1,0:T(8,128)(2,1)S(1)}, bf16[128,2304]{1,0:T(8,128)(2,1)S(1)}, u32[]{:S(2)}, u32[]{:S(2)}) collective-permute-start(bf16[128,2304]{1,0:T(8,128)(2,1)S(1)} %collective-permute-done.24), channel_id=1, source_target_pairs={{0,2},{2,0},{1,3},{3,1},{4,6},{6,4},{5,7},{7,5},{8,10},{10,8},{9,1... | collective-permute-start | bytes 1769480 | tf_op jit(solution)/shard_map/ppermute | solution.py:108
  152.1 38.3 %collective-permute-start.15 = (bf16[3,144,1152]{2,1,0:T(8,128)(2,1)S(1)}, bf16[3,144,1152]{2,1,0:T(8,128)(2,1)S(1)}, u32[]{:S(2)}, u32[]{:S(2)}) collective-permute-start(bf16[3,144,1152]{2,1,0:T(8,128)(2,1)S(1)} %get-tuple-element.7), channel_id=1, source_target_pairs={{0,12},{4,0},{8,4},{12,8},{1,13},{5,1},{9,5},{13,9},{2,14},{6,2},{... | collective-permute-start | bytes 2985992 | tf_op jit(solution)/shard_map/ppermute | solution.py:108
  162.9 12.0 %collective-permute-start.29 = (bf16[128,2304]{1,0:T(8,128)(2,1)S(1)}, bf16[128,2304]{1,0:T(8,128)(2,1)S(1)}, u32[]{:S(2)}, u32[]{:S(2)}) collective-permute-start(bf16[128,2304]{1,0:T(8,128)(2,1)S(1)} %collective-permute-done.28), channel_id=1, source_target_pairs={{0,2},{2,0},{1,3},{3,1},{4,6},{6,4},{5,7},{7,5},{8,10},{10,8},{9,1... | collective-permute-start | bytes 1769480 | tf_op jit(solution)/shard_map/ppermute | solution.py:108
  170.2 22.2 %collective-permute-start.9 = (bf16[3,144,1152]{2,1,0:T(8,128)(2,1)S(1)}, bf16[3,144,1152]{2,1,0:T(8,128)(2,1)S(1)}, u32[]{:S(2)}, u32[]{:S(2)}) collective-permute-start(bf16[3,144,1152]{2,1,0:T(8,128)(2,1)S(1)} %collective-permute-done.7), channel_id=1, source_target_pairs={{0,16},{16,0},{1,17},{17,1},{2,18},{18,2},{3,19},{19,3},{4,20},{20... | collective-permute-start | bytes 2985992 | tf_op jit(solution)/shard_map/ppermute | solution.py:108
  175.0 18.7 %copy-start.4 = (bf16[1,576,1152]{2,1,0:T(8,128)(2,1)S(1)}, bf16[1,576,1152]{2,1,0:T(8,128)(2,1)}, u32[]{:S(2)}) copy-start(bf16[1,576,1152]{2,1,0:T(8,128)(2,1)} %copy-done.3) | copy-start | bytes 3981316
  175.1 18.7 %copy-start.6 = (bf16[1,576,1152]{2,1,0:T(8,128)(2,1)S(1)}, bf16[1,576,1152]{2,1,0:T(8,128)(2,1)}, u32[]{:S(2)}) copy-start(bf16[1,576,1152]{2,1,0:T(8,128)(2,1)} %copy-done.5) | copy-start | bytes 3981316
  175.1 20.1 %collective-permute-start.8 = (bf16[3,144,1152]{2,1,0:T(8,128)(2,1)S(1)}, bf16[3,144,1152]{2,1,0:T(8,128)(2,1)S(1)}, u32[]{:S(2)}, u32[]{:S(2)}) collective-permute-start(bf16[3,144,1152]{2,1,0:T(8,128)(2,1)S(1)} %collective-permute-done.7), channel_id=1, source_target_pairs={{0,1},{1,0},{2,3},{3,2},{4,5},{5,4},{6,7},{7,6},{8,9},{9,8},{10,11... | collective-permute-start | bytes 2985992 | tf_op jit(solution)/shard_map/ppermute | solution.py:108
  175.2 61.2 %collective-permute-start.12 = (bf16[3,144,1152]{2,1,0:T(8,128)(2,1)S(1)}, bf16[3,144,1152]{2,1,0:T(8,128)(2,1)S(1)}, u32[]{:S(2)}, u32[]{:S(2)}) collective-permute-start(bf16[3,144,1152]{2,1,0:T(8,128)(2,1)S(1)} %collective-permute-done.11), channel_id=1, source_target_pairs={{0,1},{1,0},{2,3},{3,2},{4,5},{5,4},{6,7},{7,6},{8,9},{9,8},{10,11... | collective-permute-start | bytes 2985992 | tf_op jit(solution)/shard_map/ppermute | solution.py:108
  190.4 24.9 %collective-permute-start.13 = (bf16[3,144,1152]{2,1,0:T(8,128)(2,1)S(1)}, bf16[3,144,1152]{2,1,0:T(8,128)(2,1)S(1)}, u32[]{:S(2)}, u32[]{:S(2)}) collective-permute-start(bf16[3,144,1152]{2,1,0:T(8,128)(2,1)S(1)} %collective-permute-done.11), channel_id=1, source_target_pairs={{0,16},{16,0},{1,17},{17,1},{2,18},{18,2},{3,19},{19,3},{4,20},{20... | collective-permute-start | bytes 2985992 | tf_op jit(solution)/shard_map/ppermute | solution.py:108
  191.9 43.8 %collective-permute-start.17 = (bf16[3,144,1152]{2,1,0:T(8,128)(2,1)S(1)}, bf16[3,144,1152]{2,1,0:T(8,128)(2,1)S(1)}, u32[]{:S(2)}, u32[]{:S(2)}) collective-permute-start(bf16[3,144,1152]{2,1,0:T(8,128)(2,1)S(1)} %collective-permute-done.15), channel_id=1, source_target_pairs={{0,16},{16,0},{1,17},{17,1},{2,18},{18,2},{3,19},{19,3},{4,20},{20... | collective-permute-start | bytes 2985992 | tf_op jit(solution)/shard_map/ppermute | solution.py:108
  192.5 43.5 %collective-permute-start.10 = (bf16[3,144,1152]{2,1,0:T(8,128)(2,1)S(1)}, bf16[3,144,1152]{2,1,0:T(8,128)(2,1)S(1)}, u32[]{:S(2)}, u32[]{:S(2)}) collective-permute-start(bf16[3,144,1152]{2,1,0:T(8,128)(2,1)S(1)} %collective-permute-done.9), channel_id=1, source_target_pairs={{0,1},{1,0},{2,3},{3,2},{4,5},{5,4},{6,7},{7,6},{8,9},{9,8},{10,11... | collective-permute-start | bytes 2985992 | tf_op jit(solution)/shard_map/ppermute | solution.py:108
  195.2 41.8 %collective-permute-start.16 = (bf16[3,144,1152]{2,1,0:T(8,128)(2,1)S(1)}, bf16[3,144,1152]{2,1,0:T(8,128)(2,1)S(1)}, u32[]{:S(2)}, u32[]{:S(2)}) collective-permute-start(bf16[3,144,1152]{2,1,0:T(8,128)(2,1)S(1)} %collective-permute-done.15), channel_id=1, source_target_pairs={{0,1},{1,0},{2,3},{3,2},{4,5},{5,4},{6,7},{7,6},{8,9},{9,8},{10,11... | collective-permute-start | bytes 2985992 | tf_op jit(solution)/shard_map/ppermute | solution.py:108
  215.3 21.3 %collective-permute-start.14 = (bf16[3,144,1152]{2,1,0:T(8,128)(2,1)S(1)}, bf16[3,144,1152]{2,1,0:T(8,128)(2,1)S(1)}, u32[]{:S(2)}, u32[]{:S(2)}) collective-permute-start(bf16[3,144,1152]{2,1,0:T(8,128)(2,1)S(1)} %collective-permute-done.13), channel_id=1, source_target_pairs={{0,1},{1,0},{2,3},{3,2},{4,5},{5,4},{6,7},{7,6},{8,9},{9,8},{10,11... | collective-permute-start | bytes 2985992 | tf_op jit(solution)/shard_map/ppermute | solution.py:108
  235.7 2.6 collective-permute-start.18
  238.4 5.5 %copy-start.2 = (bf16[3,2304,1152]{2,1,0:T(8,128)(2,1)}, bf16[3,2304,1152]{2,1,0:T(8,128)(2,1)S(1)}, u32[]{:S(2)}) copy-start(bf16[3,2304,1152]{2,1,0:T(8,128)(2,1)S(1)} %constant_dynamic-update-slice_fusion.weights_ref) | copy-start | bytes 47775748
  254.4 37.1 %collective-permute-start.22 = (bf16[256,2304]{1,0:T(8,128)(2,1)S(1)}, bf16[256,2304]{1,0:T(8,128)(2,1)S(1)}, u32[]{:S(2)}, u32[]{:S(2)}) collective-permute-start(bf16[256,2304]{1,0:T(8,128)(2,1)S(1)} %ffn.5), channel_id=1, source_target_pairs={{2,0},{1,3},{6,4},{5,7},{10,8},{9,11},{14,12},{13,15},{18,16},{17,... | collective-permute-start | bytes 3538952 | tf_op jit(solution)/shard_map/ppermute | solution.py:245
  266.5 28.3 %collective-permute-start.26 = (bf16[256,2304]{1,0:T(8,128)(2,1)S(1)}, bf16[256,2304]{1,0:T(8,128)(2,1)S(1)}, u32[]{:S(2)}, u32[]{:S(2)}) collective-permute-start(bf16[256,2304]{1,0:T(8,128)(2,1)S(1)} %ffn.6), channel_id=1, source_target_pairs={{2,0},{1,3},{6,4},{5,7},{10,8},{9,11},{14,12},{13,15},{18,16},{17,... | collective-permute-start | bytes 3538952 | tf_op jit(solution)/shard_map/ppermute | solution.py:245
  278.2 36.6 %collective-permute-start.19 = (bf16[256,2304]{1,0:T(8,128)(2,1)S(1)}, bf16[256,2304]{1,0:T(8,128)(2,1)S(1)}, u32[]{:S(2)}, u32[]{:S(2)}) collective-permute-start(bf16[256,2304]{1,0:T(8,128)(2,1)S(1)} %ffn.4), channel_id=1, source_target_pairs={{2,0},{1,3},{6,4},{5,7},{10,8},{9,11},{14,12},{13,15},{18,16},{17,... | collective-permute-start | bytes 3538952 | tf_op jit(solution)/shard_map/ppermute | solution.py:245
  290.2 20.2 %collective-permute-start.30 = (bf16[256,2304]{1,0:T(8,128)(2,1)S(1)}, bf16[256,2304]{1,0:T(8,128)(2,1)S(1)}, u32[]{:S(2)}, u32[]{:S(2)}) collective-permute-start(bf16[256,2304]{1,0:T(8,128)(2,1)S(1)} %ffn.7), channel_id=1, source_target_pairs={{2,0},{1,3},{6,4},{5,7},{10,8},{9,11},{14,12},{13,15},{18,16},{17,... | collective-permute-start | bytes 3538952 | tf_op jit(solution)/shard_map/ppermute | solution.py:245
  292.8 43.6 %collective-permute-start.23 = (bf16[256,2304]{1,0:T(8,128)(2,1)}, bf16[256,2304]{1,0:T(8,128)(2,1)S(1)}, u32[]{:S(2)}, u32[]{:S(2)}) collective-permute-start(bf16[256,2304]{1,0:T(8,128)(2,1)} %add_convert_fusion.2), channel_id=1, source_target_pairs={{0,8},{3,11},{4,12},{7,15},{8,0},{11,3},{12,4},{15,7},{16,24},{19,... | collective-permute-start | bytes 3538952 | tf_op jit(solution)/shard_map/ppermute | solution.py:252
  296.1 40.4 %collective-permute-start.27 = (bf16[256,2304]{1,0:T(8,128)(2,1)}, bf16[256,2304]{1,0:T(8,128)(2,1)}, u32[]{:S(2)}, u32[]{:S(2)}) collective-permute-start(bf16[256,2304]{1,0:T(8,128)(2,1)} %add_convert_fusion.1), channel_id=1, source_target_pairs={{0,4},{3,7},{4,8},{7,11},{8,12},{11,15},{12,0},{15,3},{16,20},{19,... | collective-permute-start | bytes 3538952 | tf_op jit(solution)/shard_map/ppermute | solution.py:252
  311.8 37.3 %collective-permute-start.31 = (bf16[256,2304]{1,0:T(8,128)(2,1)}, bf16[256,2304]{1,0:T(8,128)(2,1)}, u32[]{:S(2)}, u32[]{:S(2)}) collective-permute-start(bf16[256,2304]{1,0:T(8,128)(2,1)} %add_convert_fusion), channel_id=1, source_target_pairs={{0,12},{3,15},{4,0},{7,3},{8,4},{11,7},{12,8},{15,11},{16,28},{19,... | collective-permute-start | bytes 3538952 | tf_op jit(solution)/shard_map/ppermute | solution.py:252
  314.8 36.9 %copy-start.8 = (bf16[256,2304]{1,0:T(8,128)(2,1)S(1)}, bf16[256,2304]{1,0:T(8,128)(2,1)}, u32[]{:S(2)}) copy-start(bf16[256,2304]{1,0:T(8,128)(2,1)} %copy-done.7) | copy-start | bytes 3538948
  314.8 36.9 %copy-start.16 = (f32[2304]{0:T(1024)S(1)}, f32[2304]{0:T(1024)}, u32[]{:S(2)}) copy-start(f32[2304]{0:T(1024)} %param.23) | copy-start | bytes 27652
  314.8 36.8 %copy-start.9 = (bf16[256,2304]{1,0:T(8,128)(2,1)}, bf16[256,2304]{1,0:T(8,128)(2,1)S(1)}, u32[]{:S(2)}) copy-start(bf16[256,2304]{1,0:T(8,128)(2,1)S(1)} %collective-permute-done.19) | copy-start | bytes 3538948
  336.5 15.2 %copy-start.10 = (bf16[256,2304]{1,0:T(8,128)(2,1)}, bf16[256,2304]{1,0:T(8,128)(2,1)S(1)}, u32[]{:S(2)}) copy-start(bf16[256,2304]{1,0:T(8,128)(2,1)S(1)} %collective-permute-done.23) | copy-start | bytes 3538948
  351.7 7.5 %copy-start.1 = (bf16[256,2304]{1,0:T(8,128)(2,1)S(1)}, bf16[256,2304]{1,0:T(8,128)(2,1)}, u32[]{:S(2)}) copy-start(bf16[256,2304]{1,0:T(8,128)(2,1)} %param.17) | copy-start | bytes 3538948
  355.3 2.9 collective-permute-start.32
